TPU v7x, 32 devices: a whole 2x2x4 slice. The times are simulated.
32 devices in a mesh: groups: 2 (over y), ulysses: 4 (over z), blk: 2 (over x), handoff: 2 (over core).
Axes of the slice: x: 2, y: 2, z: 4, core: 2. Of those that a mesh axis runs over, the one named last changes fastest.
Arguments:
- queries: bfloat16 [4, 512, 4096], P(('groups', 'handoff'), ('blk', 'ulysses')), parts along dimension 0, may hold values from -24 to 24
- keys: bfloat16 [4, 512, 2048], P(('groups', 'handoff'), ('blk', 'ulysses')), parts along dimension 0, may hold values from -7.5 to 7.5
- values: bfloat16 [4, 512, 2048], P(('groups', 'handoff'), ('blk', 'ulysses')), parts along dimension 0, may hold values from -6 to 6
- request_pages: int32 [4, 4], P('groups'), parts along dimension 0, may hold values from 1 to 4, 8 in all within a row
- page_table: int32 [4, 8], P('groups'), parts along dimension 0, may hold values from 0 to 15, as said below
Outputs:
- attended: bfloat16 [4, 512, 4096], P(('groups', 'handoff'), ('blk', 'ulysses')), parts along dimension 0
- cache_keys: bfloat16 [32, 16, 64, 128], P(('groups', 'blk', 'handoff'), 'ulysses'), parts along dimension 0
- cache_values: bfloat16 [32, 16, 64, 128], P(('groups', 'blk', 'handoff'), 'ulysses'), parts along dimension 0
There are 2 independent parts, one for each index of `groups`. A program takes and returns all parts, laid end to end along the dimension named above; each array names one. Nothing has to cross between parts.
Inputs may be any that keep to these rules, and one draw needn't show every extreme that they name: `request_pages`: A pack's 4 requests fill its 8 pages; the longest holds exactly 4 of them. `page_table`: all rows together name every pool page once; the 4 pages of each aligned run of 4 pages of a pack's row go in equal numbers to each aligned run of 4 pool pages.
All inputs are finite; a program needn't handle non-finite values.
Results may differ from a plain program's by a relative error of at most 0.012.
Values may be sent and summed in bfloat16 or wider, within the bound.
A program may use at most 64 MiB of HBM per device.

v0:
```python
import math
import jax
import jax.numpy as jnp
from jax import lax
from jax.sharding import PartitionSpec as P

QH = 32
KVH = 16
HD = 128
WINDOW = 4096
PAGE = 64
QUERY_SCALE = 144.0 ** (-0.5)
SOFT_CAP = 50.0
ROPE_BASE = 10000.0


def from_behind(block, axis, distance):
    devices = range(lax.axis_size(axis))
    route = [(i - distance, i) for i in devices if i - distance in devices]
    return lax.ppermute(block, axis, route)


def request_marks(pages_row, positions):
    request_ends = jnp.cumsum(pages_row, dtype=jnp.int32) * PAGE
    request_starts = request_ends - pages_row * PAGE
    owner_index = jnp.sum((positions[:, None] >= request_ends[None, :]).astype(jnp.int32), axis=1)
    first_token = jnp.max(
        jnp.where(positions[:, None] >= request_starts[None, :], request_starts[None, :], 0), axis=1
    )
    return (owner_index, positions - first_token)


def rotate(head_rows, offsets):
    head_width = head_rows.shape[-1]
    half_width = head_width // 2
    frequency = ROPE_BASE ** (-(2.0 * jnp.arange(half_width, dtype=jnp.float32)) / head_width)
    angles = offsets.astype(jnp.float32)[:, None] * frequency[None, :]
    cosine = jnp.cos(angles)[:, None, :]
    sines = jnp.sin(angles)[:, None, :]
    as_float = head_rows.astype(jnp.float32)
    front_half = as_float[..., :half_width]
    back_half = as_float[..., half_width:]
    turned = jnp.concatenate(
        [front_half * cosine - back_half * sines, back_half * cosine + front_half * sines], axis=-1
    )
    return turned.astype(jnp.bfloat16)


def body(queries, keys, values, request_pages, page_table):
    local_rows = queries.shape[1]
    ulysses_size = lax.axis_size("ulysses")
    blk_size = lax.axis_size("blk")
    core_count = lax.axis_size("handoff")
    pack_index = lax.axis_index("handoff")
    blk_index = lax.axis_index("blk")
    shard_rows = local_rows * ulysses_size
    window = min(WINDOW, page_table.shape[1] // 2 * PAGE)
    earlier_count = min(window // shard_rows, blk_size - 1)
    kv_local = KVH // ulysses_size
    group_size = QH // KVH
    query_split = queries[0].reshape(local_rows, ulysses_size, kv_local * group_size * HD)
    key_split = keys[0].reshape(local_rows, ulysses_size, kv_local * HD)
    value_split = values[0].reshape(local_rows, ulysses_size, kv_local * HD)
    pages_row = lax.dynamic_index_in_dim(request_pages, pack_index, 0, keepdims=False)
    positions = blk_index * shard_rows + jnp.arange(shard_rows, dtype=jnp.int32)
    query_owner, offsets = request_marks(pages_row, positions)
    queries_moved, keys_moved, values_moved = (
        lax.all_to_all(query_split, "ulysses", split_axis=1, concat_axis=0, tiled=True),
        lax.all_to_all(key_split, "ulysses", split_axis=1, concat_axis=0, tiled=True),
        lax.all_to_all(value_split, "ulysses", split_axis=1, concat_axis=0, tiled=True),
    )
    key_turned = rotate(keys_moved.reshape(shard_rows, kv_local, HD), offsets)
    local_kv = jnp.stack(
        [
            key_turned.reshape(shard_rows, kv_local * HD),
            values_moved.reshape(shard_rows, kv_local * HD),
        ]
    )
    earlier = []
    carried = local_kv
    for hop in range(earlier_count):
        carried = from_behind(carried, "blk", 1)
        earlier.append(carried)
    slots_dev = shard_rows // PAGE
    sources = blk_size * core_count
    per_peer = slots_dev // sources
    pack_row = lax.dynamic_index_in_dim(page_table, pack_index, 0, keepdims=False)
    my_pages = lax.dynamic_slice_in_dim(pack_row, blk_index * slots_dev, slots_dev)
    send_order = jnp.argsort(my_pages)
    paged = local_kv.reshape(2, slots_dev, PAGE, kv_local, HD)[:, send_order]
    paged = jnp.transpose(paged, (0, 1, 3, 2, 4))
    outgoing = paged.reshape(2, sources, per_peer, kv_local, PAGE, HD)
    received = lax.all_to_all(outgoing, ("blk", "handoff"), split_axis=1, concat_axis=1, tiled=True)
    received = received.reshape(2, slots_dev, kv_local, PAGE, HD)
    page_grid = jnp.transpose(
        page_table.reshape(core_count, blk_size, slots_dev), (1, 0, 2)
    ).reshape(sources, slots_dev)
    my_index = blk_index * core_count + pack_index
    is_here = page_grid // slots_dev == my_index
    picked = (
        jnp.sort(jnp.where(is_here, page_grid, page_table.size), axis=1)[:, :per_peer]
        - my_index * slots_dev
    )
    inverse = jnp.argsort(picked.reshape(-1))
    cache_keys = received[0][inverse]
    cache_values = received[1][inverse]
    query_turned = rotate(queries_moved.reshape(shard_rows, kv_local * group_size, HD), offsets)
    query_turned = query_turned.reshape(shard_rows, kv_local, group_size, HD)
    front_rows = window - earlier_count * shard_rows
    front_zeros = jnp.zeros((2, front_rows, kv_local * HD), jnp.bfloat16)
    table_kv = jnp.concatenate([front_zeros] + earlier[::-1] + [local_kv], axis=1)
    key_positions = (
        blk_index * shard_rows - window + jnp.arange(window + shard_rows, dtype=jnp.int32)
    )
    key_owner, unused_offsets = request_marks(pages_row, key_positions)
    block_rows = math.gcd(shard_rows, 128)
    key_span = window + block_rows

    def attend(offset):
        query_block = lax.dynamic_slice_in_dim(query_turned, offset, block_rows, 0)
        kv_block = lax.dynamic_slice_in_dim(table_kv, offset, key_span, 1)
        key_block = kv_block[0].reshape(key_span, kv_local, HD)
        value_block = kv_block[1].reshape(key_span, kv_local, HD)
        scores = (
            jnp.einsum("qgrd,kgd->gqrk", query_block, key_block, preferred_element_type=jnp.float32)
            * QUERY_SCALE
        )
        capped = SOFT_CAP * jnp.tanh(scores / SOFT_CAP)
        query_pos = lax.dynamic_slice_in_dim(positions, offset, block_rows)
        query_part = lax.dynamic_slice_in_dim(query_owner, offset, block_rows)
        key_pos = lax.dynamic_slice_in_dim(key_positions, offset, key_span)
        key_part = lax.dynamic_slice_in_dim(key_owner, offset, key_span)
        distance = query_pos[:, None] - key_pos[None, :]
        allowed = (
            (query_part[:, None] == key_part[None, :])
            & (distance >= 0)
            & (distance < window)
            & (key_pos[None, :] >= 0)
        )
        weights = jnp.where(allowed[None, :, None, :], jnp.exp(capped), jnp.float32(0.0))
        totals = jnp.sum(weights, axis=-1)
        mixture = jnp.einsum(
            "gqrk,kgd->qgrd",
            weights.astype(jnp.bfloat16),
            value_block,
            preferred_element_type=jnp.float32,
        )
        return (mixture / jnp.transpose(totals, (1, 0, 2))[..., None]).astype(jnp.bfloat16)

    starts = jnp.arange(shard_rows // block_rows, dtype=jnp.int32) * block_rows
    blocks = lax.map(attend, starts)
    outgoing_heads = blocks.reshape(ulysses_size, local_rows, 1, kv_local * group_size * HD)
    merged = lax.all_to_all(outgoing_heads, "ulysses", split_axis=0, concat_axis=2, tiled=True)
    attended = merged.reshape(1, local_rows, QH * HD)
    return (attended, cache_keys, cache_values)


def solution(mesh):
    in_specs = (
        P(("groups", "handoff"), ("blk", "ulysses"), None),
        P(("groups", "handoff"), ("blk", "ulysses"), None),
        P(("groups", "handoff"), ("blk", "ulysses"), None),
        P("groups", None),
        P("groups", None),
    )
    out_specs = (
        P(("groups", "handoff"), ("blk", "ulysses"), None),
        P(("groups", "blk", "handoff"), "ulysses", None, None),
        P(("groups", "blk", "handoff"), "ulysses", None, None),
    )
    return jax.shard_map(body, mesh=mesh, in_specs=in_specs, out_specs=out_specs, check_vma=False)
```

profile of v0, /device:TPU:0, one launch (start us, length us, event | category | flops | bytes accessed | tf_op | source)
XLA Modules:
  0.0 87.5 jit_solution(2109109784763567030)
XLA Ops:
  0.7 1.2 %reshape_squeeze.9 = bf16[64,4,512]{2,1,0:T(4,128)(2,1)S(1)} reshape(bf16[1,64,2048]{2,1,0:T(8,128)(2,1)} %param.8) | data formatting | bytes 524288 | tf_op jit(solution)/shard_map/reshape;squeeze | solution.py:62
  1.8 0.7 copy.70
  2.6 6.5 %all-to-all-start = ((bf16[64,4,512]{2,0,1:T(8,128)(2,1)}), bf16[64,4,512]{2,0,1:T(8,128)(2,1)S(1)}, u32[]{:S(2)}, u32[]{:S(2)}) async-start(bf16[64,4,512]{2,0,1:T(8,128)(2,1)} %copy.70), calls=%async_computation | async-start | bytes 524288 | tf_op jit(solution)/shard_map/all_to_all | solution.py:69
  9.5 0.7 sort.46
  10.5 0.7 copy.71
  11.4 6.6 %all-to-all-done = bf16[64,4,512]{2,0,1:T(8,128)(2,1)S(1)} async-done(((bf16[64,4,512]{2,0,1:T(8,128)(2,1)}), bf16[64,4,512]{2,0,1:T(8,128)(2,1)S(1)}, u32[]{:S(2)}, u32[]{:S(2)}) %all-to-all-start) | async-done | bytes 262176 | tf_op jit(solution)/shard_map/all_to_all | solution.py:69
  18.0 3.4 %all-to-all-start.1 = ((bf16[64,4,512]{2,0,1:T(8,128)(2,1)}), bf16[64,4,512]{2,0,1:T(8,128)(2,1)S(1)}, u32[]{:S(2)}, u32[]{:S(2)}) async-start(bf16[64,4,512]{2,0,1:T(8,128)(2,1)} %copy.71), calls=%async_computation.1 | async-start | bytes 524288 | tf_op jit(solution)/shard_map/all_to_all | solution.py:70
  21.8 1.0 %copy.72 = bf16[64,4,1024]{2,0,1:T(8,128)(2,1)} copy(bf16[64,4,1024]{2,1,0:T(4,128)(2,1)S(1)} %reshape_squeeze.11) | data formatting | bytes 1048576 | tf_op jit(solution)/shard_map/reshape;squeeze | solution.py:61
  22.8 0.6 sort.47
  23.5 0.5 multiply_cosine_fusion
  24.0 4.4 %all-to-all-done.1 = bf16[64,4,512]{2,0,1:T(8,128)(2,1)S(1)} async-done(((bf16[64,4,512]{2,0,1:T(8,128)(2,1)}), bf16[64,4,512]{2,0,1:T(8,128)(2,1)S(1)}, u32[]{:S(2)}, u32[]{:S(2)}) %all-to-all-start.1) | async-done | bytes 262176 | tf_op jit(solution)/shard_map/all_to_all | solution.py:70
  28.4 3.5 %all-to-all-start.2 = ((bf16[64,4,1024]{2,0,1:T(8,128)(2,1)}), bf16[64,4,1024]{2,0,1:T(8,128)(2,1)S(1)}, u32[]{:S(2)}, u32[]{:S(2)}) async-start(bf16[64,4,1024]{2,0,1:T(8,128)(2,1)} %copy.72), calls=%async_computation.2 | async-start | bytes 1048576 | tf_op jit(solution)/shard_map/all_to_all | solution.py:68
  33.3 4.2 %collective-permute-start = (bf16[2,256,512]{2,1,0:T(8,128)(2,1)S(1)}, bf16[2,256,512]{2,1,0:T(8,128)(2,1)}, u32[]{:S(2)}, u32[]{:S(2)}) collective-permute-start(bf16[2,256,512]{2,1,0:T(8,128)(2,1)S(1)} %pad_maximum_fusion), channel_id=1, source_target_pairs={{0,2},{1,3},{4,6},{5,7},{8,10},{9,11},{12,14},{13,15},{16,18},{17,... | collective-permute-start | bytes 1572872 | tf_op jit(solution)/shard_map/ppermute | solution.py:20
  37.6 1.4 %gather_fusion = bf16[4,2,64,4,128]{4,2,3,1,0:T(8,128)(2,1)} fusion(bf16[2,4,64,4,128]{4,2,3,1,0:T(8,128)(2,1)S(1)} %pad_maximum_fusion.2, s32[1024]{0:T(1024)S(1)} %pad_clamp_fusion.1), kind=kCustom, calls=%fused_computation | custom fusion | bytes 1048592 | tf_op jit(solution)/shard_map/gather | solution.py:90
  39.0 4.6 %all-to-all-done.2 = bf16[64,4,1024]{2,0,1:T(8,128)(2,1)S(1)} async-done(((bf16[64,4,1024]{2,0,1:T(8,128)(2,1)}), bf16[64,4,1024]{2,0,1:T(8,128)(2,1)S(1)}, u32[]{:S(2)}, u32[]{:S(2)}) %all-to-all-start.2) | async-done | bytes 524320 | tf_op jit(solution)/shard_map/all_to_all | solution.py:68
  43.6 3.5 %all-to-all-start.4 = ((bf16[2,4,1,4,64,128]{5,4,3,0,2,1:T(8,128)(2,1)}), bf16[2,4,1,4,64,128]{5,4,3,0,2,1:T(8,128)(2,1)S(1)}, u32[]{:S(2)}, u32[]{:S(2)}) async-start(bf16[2,4,1,4,64,128]{5,4,3,0,2,1:T(8,128)(2,1)} %bitcast.30), calls=%async_computation.4 | async-start | bytes 1048576 | tf_op jit(solution)/shard_map/all_to_all | solution.py:93
  47.4 0.5 subtract_convert_fusion
  48.4 1.1 %maximum_maximum_fusion = bf16[2,512,512]{2,1,0:T(8,128)(2,1)S(1)} fusion(bf16[1,256,512]{2,1,0:T(8,128)(2,1)S(1)} %bitcast.114, bf16[1,256,512]{2,1,0:T(8,128)(2,1)S(1)} %convert_element_type.81, bf16[2,256,512]{2,1,0:T(8,128)(2,1)} %collective-permute-done), kind=kLoop, calls=%fused_computation.20 | loop fusion | flops 3145728 | bytes 2097152 | tf_op jit(solution)/shard_map/concatenate | solution.py:111
  49.5 15.4 %while.12 = (s32[]{:T(128)}, bf16[2,128,4,2,128]{4,3,2,1,0:T(2,128)(2,1)}, s32[2]{0:T(128)S(1)}, bf16[2,512,512]{2,1,0:T(8,128)(2,1)S(1)}, s32[256]{0:T(256)S(1)...) while((s32[]{:T(128)}, ...), condition=%wide.region_6.7_spmd, body=%wide.region_4.6_spmd.sunk | while | flops 203898240 | bytes 11392056 | solution.py:151
  49.5 0.6 dynamic_slice.76
  54.4 0.7 fusion.29
  56.4 0.8 copy-done.2
  57.2 0.6 dynamic_slice.76
  62.1 0.7 fusion.29
  64.1 0.8 copy-done.2
  64.9 2.2 %reshape.238 = bf16[4,64,1,1024]{3,1,0,2:T(8,128)(2,1)} reshape(bf16[2,128,4,2,128]{4,3,2,1,0:T(2,128)(2,1)} %get-tuple-element.120) | data formatting | bytes 1048576 | tf_op jit(solution)/shard_map/reshape | solution.py:152
  67.1 3.5 %all-to-all-start.3 = ((bf16[4,64,1,1024]{3,1,2,0:T(8,128)(2,1)}), bf16[4,64,1,1024]{3,1,2,0:T(8,128)(2,1)S(1)}, u32[]{:S(2)}, u32[]{:S(2)}) async-start(bf16[4,64,1,1024]{3,1,2,0:T(8,128)(2,1)} %bitcast.22), calls=%async_computation.3 | async-start | bytes 1048576 | tf_op jit(solution)/shard_map/all_to_all | solution.py:153
  70.6 0.7 sort.48
  71.4 1.3 %gather_fusion.2 = bf16[4,4,64,128]{3,2,1,0:T(8,128)(2,1)} fusion(bf16[4,4,64,128]{3,2,1,0:T(8,128)(2,1)S(1)} %get-tuple-element.190, s32[1024]{0:T(1024)S(1)} %pad_clamp_fusion), kind=kCustom, calls=%fused_computation.2 | custom fusion | bytes 524304 | tf_op jit(solution)/shard_map/gather | solution.py:106
  72.7 1.3 %gather_fusion.1 = bf16[4,4,64,128]{3,2,1,0:T(8,128)(2,1)} fusion(bf16[4,4,64,128]{3,2,1,0:T(8,128)(2,1)S(1)} %get-tuple-element.191, s32[1024]{0:T(1024)S(1)} %pad_clamp_fusion), kind=kCustom, calls=%fused_computation.1 | custom fusion | bytes 524304 | tf_op jit(solution)/shard_map/gather | solution.py:105
  73.9 12.0 %all-to-all-done.3 = bf16[4,64,1,1024]{3,1,2,0:T(8,128)(2,1)S(1)} async-done(((bf16[4,64,1,1024]{3,1,2,0:T(8,128)(2,1)}), bf16[4,64,1,1024]{3,1,2,0:T(8,128)(2,1)S(1)}, u32[]{:S(2)}, u32[]{:S(2)}) %all-to-all-start.3) | async-done | bytes 524320 | tf_op jit(solution)/shard_map/all_to_all | solution.py:153
  86.3 1.2 %reshape.239 = bf16[1,64,4096]{2,1,0:T(8,128)(2,1)} reshape(bf16[1,64,4,1,1024]{4,2,1,3,0:T(4,128)(2,1)S(1)} %copy.78) | data formatting | bytes 1048576 | tf_op jit(solution)/shard_map/reshape | solution.py:154
  (82 shorter events, 8.5 us)
Async XLA Ops:
  0.6 8.4 %copy-start.5 = (s32[2,4]{1,0:T(2,128)S(1)}, s32[2,4]{1,0:T(2,128)}, u32[]{:S(2)}) copy-start(s32[2,4]{1,0:T(2,128)} %param.10) | copy-start | bytes 100
  0.6 8.7 %copy-start.4 = (s32[2,8]{1,0:T(2,128)S(1)}, s32[2,8]{1,0:T(2,128)}, u32[]{:S(2)}) copy-start(s32[2,8]{1,0:T(2,128)} %param.11) | copy-start | bytes 196
  0.7 9.7 %copy-start.3 = (bf16[1,64,2048]{2,1,0:T(8,128)(2,1)S(1)}, bf16[1,64,2048]{2,1,0:T(8,128)(2,1)}, u32[]{:S(2)}) copy-start(bf16[1,64,2048]{2,1,0:T(8,128)(2,1)} %param.9) | copy-start | bytes 786436
  2.6 18.8 %copy-start = (bf16[1,64,4096]{2,1,0:T(8,128)(2,1)S(1)}, bf16[1,64,4096]{2,1,0:T(8,128)(2,1)}, u32[]{:S(2)}) copy-start(bf16[1,64,4096]{2,1,0:T(8,128)(2,1)} %param.7) | copy-start | bytes 1572868
  2.6 15.4 %all-to-all-start = ((bf16[64,4,512]{2,0,1:T(8,128)(2,1)}), bf16[64,4,512]{2,0,1:T(8,128)(2,1)S(1)}, u32[]{:S(2)}, u32[]{:S(2)}) async-start(bf16[64,4,512]{2,0,1:T(8,128)(2,1)} %copy.70), calls=%async_computation | async-start | bytes 524288 | tf_op jit(solution)/shard_map/all_to_all | solution.py:69
  18.0 10.4 %all-to-all-start.1 = ((bf16[64,4,512]{2,0,1:T(8,128)(2,1)}), bf16[64,4,512]{2,0,1:T(8,128)(2,1)S(1)}, u32[]{:S(2)}, u32[]{:S(2)}) async-start(bf16[64,4,512]{2,0,1:T(8,128)(2,1)} %copy.71), calls=%async_computation.1 | async-start | bytes 524288 | tf_op jit(solution)/shard_map/all_to_all | solution.py:70
  28.4 15.2 %all-to-all-start.2 = ((bf16[64,4,1024]{2,0,1:T(8,128)(2,1)}), bf16[64,4,1024]{2,0,1:T(8,128)(2,1)S(1)}, u32[]{:S(2)}, u32[]{:S(2)}) async-start(bf16[64,4,1024]{2,0,1:T(8,128)(2,1)} %copy.72), calls=%async_computation.2 | async-start | bytes 1048576 | tf_op jit(solution)/shard_map/all_to_all | solution.py:68
  33.3 15.0 %collective-permute-start = (bf16[2,256,512]{2,1,0:T(8,128)(2,1)S(1)}, bf16[2,256,512]{2,1,0:T(8,128)(2,1)}, u32[]{:S(2)}, u32[]{:S(2)}) collective-permute-start(bf16[2,256,512]{2,1,0:T(8,128)(2,1)S(1)} %pad_maximum_fusion), channel_id=1, source_target_pairs={{0,2},{1,3},{4,6},{5,7},{8,10},{9,11},{12,14},{13,15},{16,18},{17,... | collective-permute-start | bytes 1572872 | tf_op jit(solution)/shard_map/ppermute | solution.py:20
  43.6 23.5 %all-to-all-start.4 = ((bf16[2,4,1,4,64,128]{5,4,3,0,2,1:T(8,128)(2,1)}), bf16[2,4,1,4,64,128]{5,4,3,0,2,1:T(8,128)(2,1)S(1)}, u32[]{:S(2)}, u32[]{:S(2)}) async-start(bf16[2,4,1,4,64,128]{5,4,3,0,2,1:T(8,128)(2,1)} %bitcast.30), calls=%async_computation.4 | async-start | bytes 1048576 | tf_op jit(solution)/shard_map/all_to_all | solution.py:93
  55.1 1.0 %copy-start.1 = (bf16[2,128,4,2,128]{4,3,2,1,0:T(2,128)(2,1)S(1)}, bf16[2,128,4,2,128]{4,3,2,1,0:T(2,128)(2,1)}, u32[]{:S(2)}) copy-start(bf16[2,128,4,2,128]{4,3,2,1,0:T(2,128)(2,1)} %get-tuple-element.278) | copy-start | bytes 1572868 | tf_op jit(solution)/shard_map/while
  56.4 0.8 copy-start.2
  62.8 1.0 %copy-start.1 = (bf16[2,128,4,2,128]{4,3,2,1,0:T(2,128)(2,1)S(1)}, bf16[2,128,4,2,128]{4,3,2,1,0:T(2,128)(2,1)}, u32[]{:S(2)}) copy-start(bf16[2,128,4,2,128]{4,3,2,1,0:T(2,128)(2,1)} %get-tuple-element.278) | copy-start | bytes 1572868 | tf_op jit(solution)/shard_map/while
  64.1 0.8 copy-start.2
  67.1 18.8 %all-to-all-start.3 = ((bf16[4,64,1,1024]{3,1,2,0:T(8,128)(2,1)}), bf16[4,64,1,1024]{3,1,2,0:T(8,128)(2,1)S(1)}, u32[]{:S(2)}, u32[]{:S(2)}) async-start(bf16[4,64,1,1024]{3,1,2,0:T(8,128)(2,1)} %bitcast.22), calls=%async_computation.3 | async-start | bytes 1048576 | tf_op jit(solution)/shard_map/all_to_all | solution.py:153
where the time goes:
time: 88.3 us; the launch traced here: 87.5 us
  waiting for transfers between devices  27.5 us (31%)
  starting transfers between devices  24.5 us (28%)
  local copies, waits for them, and re-layouts  19.2 us (22%)
  loops' own time  6.61 us (7%)
  other arithmetic  6.52 us (7%)
  matrix products  2.22 us (3%)
  between operations  0.94 us (1%)
    all_to_all x1, waiting for transfers between devices, body(): lax.all_to_all(outgoing_heads, 'ulysses', split_axis=0, concat_axis=2, ti...  12 us
    another operation x1, loops' own time, body(): blocks = lax.map(attend, starts)  6.61 us
    all_to_all x1, waiting for transfers between devices, body(): lax.all_to_all(key_split, 'ulysses', split_axis=1, concat_axis=0, tiled=T...  6.59 us
    all_to_all x1, starting transfers between devices, body(): lax.all_to_all(key_split, 'ulysses', split_axis=1, concat_axis=0, tiled=T...  6.48 us
    all_to_all x1, waiting for transfers between devices, body(): lax.all_to_all(query_split, 'ulysses', split_axis=1, concat_axis=0, tiled...  4.61 us
    all_to_all x1, waiting for transfers between devices, body(): lax.all_to_all(value_split, 'ulysses', split_axis=1, concat_axis=0, tiled...  4.36 us
    ppermute x1, starting transfers between devices, from_behind(): return lax.ppermute(block, axis, route)  4.21 us
    all_to_all x1, starting transfers between devices, body(): lax.all_to_all(outgoing_heads, 'ulysses', split_axis=0, concat_axis=2, ti...  3.47 us
  transfers between devices with their start and end apart: 6, of which 4 were waited for; matrix products, arithmetic and copies ran while one was open for 25% of the time, Pallas kernels for 0%

commit v1 on v0

--- a/solution.py
+++ b/solution.py
@@ -12,6 +12,18 @@
 QUERY_SCALE = 144.0 ** (-0.5)
 SOFT_CAP = 50.0
 ROPE_BASE = 10000.0
+
+
+def exchange_directly(x, axis, split, join):
+    ways, here = (lax.axis_size(axis), lax.axis_index(axis))
+    width = x.shape[split] // ways
+    turned = jnp.roll(x, -here * width, axis=split)
+    got = [lax.slice_in_dim(turned, 0, width, axis=split)]
+    for far in range(1, ways):
+        sent = lax.slice_in_dim(turned, far * width, (far + 1) * width, axis=split)
+        got.append(lax.ppermute(sent, axis, [(d, (d + far) % ways) for d in range(ways)]))
+    line = jnp.concatenate(got[::-1], axis=join)
+    return jnp.roll(line, (here + 1) * got[0].shape[join], axis=join)
 
 
 def from_behind(block, axis, distance):
@@ -66,7 +78,7 @@
     query_owner, offsets = request_marks(pages_row, positions)
     queries_moved, keys_moved, values_moved = (
         lax.all_to_all(query_split, "ulysses", split_axis=1, concat_axis=0, tiled=True),
-        lax.all_to_all(key_split, "ulysses", split_axis=1, concat_axis=0, tiled=True),
+        exchange_directly(key_split, "ulysses", 1, 0),
         lax.all_to_all(value_split, "ulysses", split_axis=1, concat_axis=0, tiled=True),
     )
     key_turned = rotate(keys_moved.reshape(shard_rows, kv_local, HD), offsets)

time: 88.3 us -> 92.2 us (1.044)
  starting transfers between devices: 24.5 us -> 27.9 us
  local copies, waits for them, and re-layouts: 19.2 us -> 20.6 us
  waiting for transfers between devices: 27.5 us -> 26.1 us
    ppermute x0 -> x3, waiting for transfers between devices: none -> 7.21 us  [exchange_directly(): lax.ppermute(sent, axis, [(d, (d + far) % ways) for d in range(ways)])]
    all_to_all x1 -> x0, waiting for transfers between devices: 6.59 us -> none  [body(): lax.all_to_all(key_split, 'ulysses', split_axis=1, concat_axis=0, tiled=T...]
    all_to_all x1 -> x0, starting transfers between devices: 6.48 us -> none  [body(): lax.all_to_all(key_split, 'ulysses', split_axis=1, concat_axis=0, tiled=T...]
    ppermute x0 -> x3, starting transfers between devices: none -> 5.9 us  [exchange_directly(): lax.ppermute(sent, axis, [(d, (d + far) % ways) for d in range(ways)])]
    all_to_all x1, waiting for transfers between devices: 4.36 us -> 0.01 us  [body(): lax.all_to_all(value_split, 'ulysses', split_axis=1, concat_axis=0, tiled...]
    all_to_all x1, waiting for transfers between devices: 4.61 us -> 7.59 us  [body(): lax.all_to_all(query_split, 'ulysses', split_axis=1, concat_axis=0, tiled...]
    all_to_all x1, starting transfers between devices: 3.41 us -> 6.35 us  [body(): lax.all_to_all(value_split, 'ulysses', split_axis=1, concat_axis=0, tiled...]
    another operation x3 -> x1, local copies, waits for them, and re-layouts: 1.93 us -> 0.01 us  [the longest x2 1.93 us: body(): key_split = keys[0].reshape(local_rows, ulysses_size, kv_local * HD)]
  transfers between devices with their start and end apart: 6 -> 8, of which waited for: 4 -> 4; matrix products, arithmetic and copies ran while one was open for 25% -> 26% of each run, Pallas kernels for 0% -> 0%
where the time goes in v1:
time: 92.2 us; the launch traced here: 91.5 us
  starting transfers between devices  27.9 us (30%)
  waiting for transfers between devices  26.1 us (28%)
  local copies, waits for them, and re-layouts  20.6 us (22%)
  other arithmetic  7.04 us (8%)
  loops' own time  6.61 us (7%)
  matrix products  2.23 us (2%)
  between operations  0.99 us (1%)
    all_to_all x1, waiting for transfers between devices, body(): lax.all_to_all(outgoing_heads, 'ulysses', split_axis=0, concat_axis=2, ti...  11.3 us
    all_to_all x1, waiting for transfers between devices, body(): lax.all_to_all(query_split, 'ulysses', split_axis=1, concat_axis=0, tiled...  7.59 us
    ppermute x3, waiting for transfers between devices, exchange_directly(): lax.ppermute(sent, axis, [(d, (d + far) % ways) for d in range(ways)])  7.21 us
    another operation x1, loops' own time, body(): blocks = lax.map(attend, starts)  6.61 us
    all_to_all x1, starting transfers between devices, body(): lax.all_to_all(value_split, 'ulysses', split_axis=1, concat_axis=0, tiled...  6.35 us
    ppermute x3, starting transfers between devices, exchange_directly(): lax.ppermute(sent, axis, [(d, (d + far) % ways) for d in range(ways)])  5.9 us
    all_to_all x1, starting transfers between devices, body(): lax.all_to_all(query_split, 'ulysses', split_axis=1, concat_axis=0, tiled...  4.52 us
    ppermute x1, starting transfers between devices, from_behind(): return lax.ppermute(block, axis, route)  4.22 us
  transfers between devices with their start and end apart: 8, of which 4 were waited for; matrix products, arithmetic and copies ran while one was open for 26% of the time, Pallas kernels for 0%

profile of v1, /device:TPU:0, one launch (start us, length us, event | category | flops | bytes accessed | tf_op | source)
XLA Modules:
  0.0 91.5 jit_solution(4448681678967332824)
XLA Ops:
  0.6 1.2 %reshape_squeeze.10 = bf16[64,4,512]{2,1,0:T(4,128)(2,1)S(1)} reshape(bf16[1,64,2048]{2,1,0:T(8,128)(2,1)} %param.9) | data formatting | bytes 524288 | tf_op jit(solution)/shard_map/reshape;squeeze | solution.py:75
  1.8 0.7 copy.76
  2.6 6.3 %all-to-all-start = ((bf16[64,4,512]{2,0,1:T(8,128)(2,1)}), bf16[64,4,512]{2,0,1:T(8,128)(2,1)S(1)}, u32[]{:S(2)}, u32[]{:S(2)}) async-start(bf16[64,4,512]{2,0,1:T(8,128)(2,1)} %copy.76), calls=%async_computation | async-start | bytes 524288 | tf_op jit(solution)/shard_map/all_to_all | solution.py:82
  9.6 2.1 %collective-permute-start.2 = (bf16[64,1,512]{0,2,1:T(8,128)(2,1)S(1)}, bf16[64,1,512]{0,2,1:T(8,128)(2,1)S(1)}, u32[]{:S(2)}, u32[]{:S(2)}) collective-permute-start(bf16[64,1,512]{0,2,1:T(8,128)(2,1)S(1)} %get-tuple-element.193), channel_id=1, source_target_pairs={{0,4},{4,8},{8,12},{12,0},{1,5},{5,9},{9,13},{13,1},{2,6},{6,10},{... | collective-permute-start | bytes 196616 | tf_op jit(solution)/shard_map/ppermute | solution.py:24
  11.6 2.4 %collective-permute-start.1 = (bf16[64,1,512]{0,2,1:T(8,128)(2,1)S(1)}, bf16[64,1,512]{0,2,1:T(8,128)(2,1)S(1)}, u32[]{:S(2)}, u32[]{:S(2)}) collective-permute-start(bf16[64,1,512]{0,2,1:T(8,128)(2,1)S(1)} %get-tuple-element.194), channel_id=1, source_target_pairs={{0,8},{4,12},{8,0},{12,4},{1,9},{5,13},{9,1},{13,5},{2,10},{6,14},... | collective-permute-start | bytes 196616 | tf_op jit(solution)/shard_map/ppermute | solution.py:24
  14.0 1.5 %collective-permute-start = (bf16[64,1,512]{0,2,1:T(8,128)(2,1)S(1)}, bf16[64,1,512]{0,2,1:T(8,128)(2,1)S(1)}, u32[]{:S(2)}, u32[]{:S(2)}) collective-permute-start(bf16[64,1,512]{0,2,1:T(8,128)(2,1)S(1)} %get-tuple-element.195), channel_id=1, source_target_pairs={{0,12},{4,0},{8,4},{12,8},{1,13},{5,1},{9,5},{13,9},{2,14},{6,2},{... | collective-permute-start | bytes 196616 | tf_op jit(solution)/shard_map/ppermute | solution.py:24
  15.9 0.7 sort.46
  17.8 1.0 %copy.78 = bf16[64,4,1024]{2,0,1:T(8,128)(2,1)} copy(bf16[64,4,1024]{2,1,0:T(4,128)(2,1)S(1)} %reshape_squeeze.11) | data formatting | bytes 1048576 | tf_op jit(solution)/shard_map/reshape;squeeze | solution.py:73
  18.8 0.6 sort.47
  20.0 1.5 %collective-permute-done.2 = bf16[64,1,512]{0,2,1:T(8,128)(2,1)S(1)} collective-permute-done((bf16[64,1,512]{0,2,1:T(8,128)(2,1)S(1)}, bf16[64,1,512]{0,2,1:T(8,128)(2,1)S(1)}, u32[]{:S(2)}, u32[]{:S(2)}) %collective-permute-start.2) | collective-permute-done | bytes 65568 | tf_op jit(solution)/shard_map/ppermute | solution.py:24
  21.5 5.7 %collective-permute-done.1 = bf16[64,1,512]{0,2,1:T(8,128)(2,1)S(1)} collective-permute-done((bf16[64,1,512]{0,2,1:T(8,128)(2,1)S(1)}, bf16[64,1,512]{0,2,1:T(8,128)(2,1)S(1)}, u32[]{:S(2)}, u32[]{:S(2)}) %collective-permute-start.1) | collective-permute-done | bytes 65568 | tf_op jit(solution)/shard_map/ppermute | solution.py:24
  27.7 4.5 %all-to-all-start.1 = ((bf16[64,4,1024]{2,0,1:T(8,128)(2,1)}), bf16[64,4,1024]{2,0,1:T(8,128)(2,1)S(1)}, u32[]{:S(2)}, u32[]{:S(2)}) async-start(bf16[64,4,1024]{2,0,1:T(8,128)(2,1)} %copy.78), calls=%async_computation.1 | async-start | bytes 1048576 | tf_op jit(solution)/shard_map/all_to_all | solution.py:80
  33.1 4.2 %collective-permute-start.3 = (bf16[2,256,512]{2,1,0:T(8,128)(2,1)S(1)}, bf16[2,256,512]{2,1,0:T(8,128)(2,1)}, u32[]{:S(2)}, u32[]{:S(2)}) collective-permute-start(bf16[2,256,512]{2,1,0:T(8,128)(2,1)S(1)} %pad_maximum_fusion), channel_id=1, source_target_pairs={{0,2},{1,3},{4,6},{5,7},{8,10},{9,11},{12,14},{13,15},{16,18},{17,... | collective-permute-start | bytes 1572872 | tf_op jit(solution)/shard_map/ppermute | solution.py:32
  37.3 1.4 %gather_fusion = bf16[4,2,64,4,128]{4,2,3,1,0:T(8,128)(2,1)} fusion(bf16[2,4,64,4,128]{4,2,3,1,0:T(8,128)(2,1)S(1)} %pad_maximum_fusion.2, s32[1024]{0:T(1024)S(1)} %pad_clamp_fusion.1), kind=kCustom, calls=%fused_computation | custom fusion | bytes 1048592 | tf_op jit(solution)/shard_map/gather | solution.py:102
  38.7 7.6 %all-to-all-done.1 = bf16[64,4,1024]{2,0,1:T(8,128)(2,1)S(1)} async-done(((bf16[64,4,1024]{2,0,1:T(8,128)(2,1)}), bf16[64,4,1024]{2,0,1:T(8,128)(2,1)S(1)}, u32[]{:S(2)}, u32[]{:S(2)}) %all-to-all-start.1) | async-done | bytes 524320 | tf_op jit(solution)/shard_map/all_to_all | solution.py:80
  46.3 3.5 %all-to-all-start.3 = ((bf16[2,4,1,4,64,128]{5,4,3,0,2,1:T(8,128)(2,1)}), bf16[2,4,1,4,64,128]{5,4,3,0,2,1:T(8,128)(2,1)S(1)}, u32[]{:S(2)}, u32[]{:S(2)}) async-start(bf16[2,4,1,4,64,128]{5,4,3,0,2,1:T(8,128)(2,1)} %bitcast.32), calls=%async_computation.3 | async-start | bytes 1048576 | tf_op jit(solution)/shard_map/all_to_all | solution.py:105
  51.1 1.1 %maximum_maximum_fusion = bf16[2,512,512]{2,1,0:T(8,128)(2,1)S(1)} fusion(bf16[1,256,512]{2,1,0:T(8,128)(2,1)S(1)} %bitcast.109, bf16[1,256,512]{2,1,0:T(8,128)(2,1)S(1)} %copy.77, bf16[2,256,512]{2,1,0:T(8,128)(2,1)} %collective-permute-done.3), kind=kLoop, calls=%fused_computation.22 | loop fusion | flops 3145728 | bytes 2097152 | tf_op jit(solution)/shard_map/concatenate | solution.py:123
  52.2 16.6 %while.12 = (s32[]{:T(128)}, bf16[2,128,4,2,128]{4,3,2,1,0:T(2,128)(2,1)}, s32[2]{0:T(128)}, bf16[2,512,512]{2,1,0:T(8,128)(2,1)S(1)}, s32[256]{0:T(256)S(1)}, /...) while((s32[]{:T(128)}, ...), condition=%wide.region_6.7_spmd, body=%wide.region_4.6_spmd.sunk | while | flops 203898240 | bytes 11392056 | solution.py:163
  52.2 1.2 %dynamic_slice.95 = s32[1]{0:T(128)} dynamic-slice(s32[2]{0:T(128)} %get-tuple-element.297, s32[]{:T(128)S(6)} %copy.122), dynamic_slice_sizes={1} | dynamic-slice | bytes 12 | tf_op jit(solution)/shard_map/while/body/jit(dynamic_index_in_dim)/dynamic_slice | solution.py:163
  57.8 0.7 fusion.32
  59.8 0.8 copy-done.2
  60.6 1.2 %dynamic_slice.95 = s32[1]{0:T(128)} dynamic-slice(s32[2]{0:T(128)} %get-tuple-element.297, s32[]{:T(128)S(6)} %copy.122), dynamic_slice_sizes={1} | dynamic-slice | bytes 12 | tf_op jit(solution)/shard_map/while/body/jit(dynamic_index_in_dim)/dynamic_slice | solution.py:163
  66.1 0.7 fusion.32
  68.1 0.8 copy-done.2
  68.9 2.2 %reshape.235 = bf16[4,64,1,1024]{3,1,0,2:T(8,128)(2,1)} reshape(bf16[2,128,4,2,128]{4,3,2,1,0:T(2,128)(2,1)} %get-tuple-element.120) | data formatting | bytes 1048576 | tf_op jit(solution)/shard_map/reshape | solution.py:164
  71.1 3.5 %all-to-all-start.2 = ((bf16[4,64,1,1024]{3,1,2,0:T(8,128)(2,1)}), bf16[4,64,1,1024]{3,1,2,0:T(8,128)(2,1)S(1)}, u32[]{:S(2)}, u32[]{:S(2)}) async-start(bf16[4,64,1,1024]{3,1,2,0:T(8,128)(2,1)} %bitcast.24), calls=%async_computation.2 | async-start | bytes 1048576 | tf_op jit(solution)/shard_map/all_to_all | solution.py:165
  74.6 0.7 subtract_bitcast_fusion
  75.3 0.7 sort.48
  76.1 1.3 %gather_fusion.2 = bf16[4,4,64,128]{3,2,1,0:T(8,128)(2,1)} fusion(bf16[4,4,64,128]{3,2,1,0:T(8,128)(2,1)S(1)} %get-tuple-element.190, s32[1024]{0:T(1024)S(1)} %pad_clamp_fusion), kind=kCustom, calls=%fused_computation.2 | custom fusion | bytes 524304 | tf_op jit(solution)/shard_map/gather | solution.py:118
  77.3 1.3 %gather_fusion.1 = bf16[4,4,64,128]{3,2,1,0:T(8,128)(2,1)} fusion(bf16[4,4,64,128]{3,2,1,0:T(8,128)(2,1)S(1)} %get-tuple-element.191, s32[1024]{0:T(1024)S(1)} %pad_clamp_fusion), kind=kCustom, calls=%fused_computation.1 | custom fusion | bytes 524304 | tf_op jit(solution)/shard_map/gather | solution.py:117
  78.6 11.3 %all-to-all-done.2 = bf16[4,64,1,1024]{3,1,2,0:T(8,128)(2,1)S(1)} async-done(((bf16[4,64,1,1024]{3,1,2,0:T(8,128)(2,1)}), bf16[4,64,1,1024]{3,1,2,0:T(8,128)(2,1)S(1)}, u32[]{:S(2)}, u32[]{:S(2)}) %all-to-all-start.2) | async-done | bytes 524320 | tf_op jit(solution)/shard_map/all_to_all | solution.py:165
  90.3 1.2 %reshape.236 = bf16[1,64,4096]{2,1,0:T(8,128)(2,1)} reshape(bf16[1,64,4,1,1024]{4,2,1,3,0:T(4,128)(2,1)S(1)} %copy.86) | data formatting | bytes 1048576 | tf_op jit(solution)/shard_map/reshape | solution.py:166
  (90 shorter events, 10.2 us)
Async XLA Ops:
  0.6 8.3 %copy-start.3 = (bf16[1,64,2048]{2,1,0:T(8,128)(2,1)S(1)}, bf16[1,64,2048]{2,1,0:T(8,128)(2,1)}, u32[]{:S(2)}) copy-start(bf16[1,64,2048]{2,1,0:T(8,128)(2,1)} %param.8) | copy-start | bytes 786436
  2.6 25.2 %all-to-all-start = ((bf16[64,4,512]{2,0,1:T(8,128)(2,1)}), bf16[64,4,512]{2,0,1:T(8,128)(2,1)S(1)}, u32[]{:S(2)}, u32[]{:S(2)}) async-start(bf16[64,4,512]{2,0,1:T(8,128)(2,1)} %copy.76), calls=%async_computation | async-start | bytes 524288 | tf_op jit(solution)/shard_map/all_to_all | solution.py:82
  9.2 6.3 %copy-start.5 = (s32[2,4]{1,0:T(2,128)S(1)}, s32[2,4]{1,0:T(2,128)}, u32[]{:S(2)}) copy-start(s32[2,4]{1,0:T(2,128)} %param.10) | copy-start | bytes 100
  9.2 6.5 %copy-start.4 = (s32[2,8]{1,0:T(2,128)S(1)}, s32[2,8]{1,0:T(2,128)}, u32[]{:S(2)}) copy-start(s32[2,8]{1,0:T(2,128)} %param.11) | copy-start | bytes 196
  9.5 7.9 %copy-start = (bf16[1,64,4096]{2,1,0:T(8,128)(2,1)S(1)}, bf16[1,64,4096]{2,1,0:T(8,128)(2,1)}, u32[]{:S(2)}) copy-start(bf16[1,64,4096]{2,1,0:T(8,128)(2,1)} %param.7) | copy-start | bytes 1572868
  9.6 12.0 %collective-permute-start.2 = (bf16[64,1,512]{0,2,1:T(8,128)(2,1)S(1)}, bf16[64,1,512]{0,2,1:T(8,128)(2,1)S(1)}, u32[]{:S(2)}, u32[]{:S(2)}) collective-permute-start(bf16[64,1,512]{0,2,1:T(8,128)(2,1)S(1)} %get-tuple-element.193), channel_id=1, source_target_pairs={{0,4},{4,8},{8,12},{12,0},{1,5},{5,9},{9,13},{13,1},{2,6},{6,10},{... | collective-permute-start | bytes 196616 | tf_op jit(solution)/shard_map/ppermute | solution.py:24
  11.6 15.6 %collective-permute-start.1 = (bf16[64,1,512]{0,2,1:T(8,128)(2,1)S(1)}, bf16[64,1,512]{0,2,1:T(8,128)(2,1)S(1)}, u32[]{:S(2)}, u32[]{:S(2)}) collective-permute-start(bf16[64,1,512]{0,2,1:T(8,128)(2,1)S(1)} %get-tuple-element.194), channel_id=1, source_target_pairs={{0,8},{4,12},{8,0},{12,4},{1,9},{5,13},{9,1},{13,5},{2,10},{6,14},... | collective-permute-start | bytes 196616 | tf_op jit(solution)/shard_map/ppermute | solution.py:24
  14.0 13.2 %collective-permute-start = (bf16[64,1,512]{0,2,1:T(8,128)(2,1)S(1)}, bf16[64,1,512]{0,2,1:T(8,128)(2,1)S(1)}, u32[]{:S(2)}, u32[]{:S(2)}) collective-permute-start(bf16[64,1,512]{0,2,1:T(8,128)(2,1)S(1)} %get-tuple-element.195), channel_id=1, source_target_pairs={{0,12},{4,0},{8,4},{12,8},{1,13},{5,1},{9,5},{13,9},{2,14},{6,2},{... | collective-permute-start | bytes 196616 | tf_op jit(solution)/shard_map/ppermute | solution.py:24
  27.7 18.6 %all-to-all-start.1 = ((bf16[64,4,1024]{2,0,1:T(8,128)(2,1)}), bf16[64,4,1024]{2,0,1:T(8,128)(2,1)S(1)}, u32[]{:S(2)}, u32[]{:S(2)}) async-start(bf16[64,4,1024]{2,0,1:T(8,128)(2,1)} %copy.78), calls=%async_computation.1 | async-start | bytes 1048576 | tf_op jit(solution)/shard_map/all_to_all | solution.py:80
  33.1 18.0 %collective-permute-start.3 = (bf16[2,256,512]{2,1,0:T(8,128)(2,1)S(1)}, bf16[2,256,512]{2,1,0:T(8,128)(2,1)}, u32[]{:S(2)}, u32[]{:S(2)}) collective-permute-start(bf16[2,256,512]{2,1,0:T(8,128)(2,1)S(1)} %pad_maximum_fusion), channel_id=1, source_target_pairs={{0,2},{1,3},{4,6},{5,7},{8,10},{9,11},{12,14},{13,15},{16,18},{17,... | collective-permute-start | bytes 1572872 | tf_op jit(solution)/shard_map/ppermute | solution.py:32
  46.3 24.8 %all-to-all-start.3 = ((bf16[2,4,1,4,64,128]{5,4,3,0,2,1:T(8,128)(2,1)}), bf16[2,4,1,4,64,128]{5,4,3,0,2,1:T(8,128)(2,1)S(1)}, u32[]{:S(2)}, u32[]{:S(2)}) async-start(bf16[2,4,1,4,64,128]{5,4,3,0,2,1:T(8,128)(2,1)} %bitcast.32), calls=%async_computation.3 | async-start | bytes 1048576 | tf_op jit(solution)/shard_map/all_to_all | solution.py:105
  58.5 1.0 %copy-start.1 = (bf16[2,128,4,2,128]{4,3,2,1,0:T(2,128)(2,1)S(1)}, bf16[2,128,4,2,128]{4,3,2,1,0:T(2,128)(2,1)}, u32[]{:S(2)}) copy-start(bf16[2,128,4,2,128]{4,3,2,1,0:T(2,128)(2,1)} %get-tuple-element.282) | copy-start | bytes 1572868 | tf_op jit(solution)/shard_map/while
  59.8 0.8 copy-start.2
  66.8 1.0 %copy-start.1 = (bf16[2,128,4,2,128]{4,3,2,1,0:T(2,128)(2,1)S(1)}, bf16[2,128,4,2,128]{4,3,2,1,0:T(2,128)(2,1)}, u32[]{:S(2)}) copy-start(bf16[2,128,4,2,128]{4,3,2,1,0:T(2,128)(2,1)} %get-tuple-element.282) | copy-start | bytes 1572868 | tf_op jit(solution)/shard_map/while
  68.1 0.8 copy-start.2
  71.1 18.8 %all-to-all-start.2 = ((bf16[4,64,1,1024]{3,1,2,0:T(8,128)(2,1)}), bf16[4,64,1,1024]{3,1,2,0:T(8,128)(2,1)S(1)}, u32[]{:S(2)}, u32[]{:S(2)}) async-start(bf16[4,64,1,1024]{3,1,2,0:T(8,128)(2,1)} %bitcast.24), calls=%async_computation.2 | async-start | bytes 1048576 | tf_op jit(solution)/shard_map/all_to_all | solution.py:165
